TPU v7x, 32 devices: a whole 2x2x4 slice. The times are simulated.
32 devices in a mesh: dp: 2 (over core), row: 4 (over y, x), col: 4 (over z).
Axes of the slice: x: 2, y: 2, z: 4, core: 2. Of those that a mesh axis runs over, the one named last changes fastest.
Arguments:
- block_input: float32 [1024, 1024], P(('dp', 'col'), 'row'), may hold values from -36 to 36
- out_cot: float32 [1024, 1024], P(('dp', 'col'), 'row'), may hold values from -6 to 6
- proj_weight: float32 [1024, 3, 1024], P('row', None, ('dp', 'col')), may hold values from -0.1875 to 0.1875
- conv_weight: float32 [3, 1024], P(None, ('dp', 'col')), may hold values from -3.5 to 3.5
- mixer_weight: float32 [1024, 1024], P(('dp', 'col'), 'row'), may hold values from -0.1875 to 0.1875
- up_weight: float32 [1024, 2, 4608], P('row', None, ('dp', 'col')), may hold values from -0.1875 to 0.1875
- down_weight: float32 [4608, 1024], P(('dp', 'col'), 'row'), may hold values from -0.09375 to 0.09375
- norm_gains: float32 [2, 1024], P(None, 'row'), may hold values from 0.25 to 1.75
- proj_moments: float32 [2, 1024, 3, 1024], P(None, 'row', None, ('dp', 'col')), may hold values from -1024 to 1024, as said below
- conv_moments: float32 [2, 3, 1024], P(None, None, ('dp', 'col')), may hold values from -1024 to 1024, as said below
- mixer_moments: float32 [2, 1024, 1024], P(None, ('dp', 'col'), 'row'), may hold values from -1024 to 1024, as said below
- up_moments: float32 [2, 1024, 2, 4608], P(None, 'row', None, ('dp', 'col')), may hold values from -1024 to 1024, as said below
- down_moments: float32 [2, 4608, 1024], P(None, ('dp', 'col'), 'row'), may hold values from -1024 to 1024, as said below
- gains_moments: float32 [2, 2, 1024], P(None, None, 'row'), may hold values from -1024 to 1024, as said below
Outputs:
- block_output: float32 [1024, 1024], P(('dp', 'col'), 'row')
- input_grad: float32 [1024, 1024], P(('dp', 'col'), 'row')
- proj_grad: float32 [1024, 3, 1024], P('row', None, ('dp', 'col'))
- conv_grad: float32 [3, 1024], P(None, ('dp', 'col'))
- mixer_grad: float32 [1024, 1024], P(('dp', 'col'), 'row')
- up_grad: float32 [1024, 2, 4608], P('row', None, ('dp', 'col'))
- down_grad: float32 [4608, 1024], P(('dp', 'col'), 'row')
- gains_grad: float32 [2, 1024], P(None, 'row')
- proj_new: float32 [1024, 3, 1024], P('row', None, ('dp', 'col'))
- conv_new: float32 [3, 1024], P(None, ('dp', 'col'))
- mixer_new: float32 [1024, 1024], P(('dp', 'col'), 'row')
- up_new: float32 [1024, 2, 4608], P('row', None, ('dp', 'col'))
- down_new: float32 [4608, 1024], P(('dp', 'col'), 'row')
- gains_new: float32 [2, 1024], P(None, 'row')
- proj_moments_new: float32 [2, 1024, 3, 1024], P(None, 'row', None, ('dp', 'col'))
- conv_moments_new: float32 [2, 3, 1024], P(None, None, ('dp', 'col'))
- mixer_moments_new: float32 [2, 1024, 1024], P(None, ('dp', 'col'), 'row')
- up_moments_new: float32 [2, 1024, 2, 4608], P(None, 'row', None, ('dp', 'col'))
- down_moments_new: float32 [2, 4608, 1024], P(None, ('dp', 'col'), 'row')
- gains_moments_new: float32 [2, 2, 1024], P(None, None, 'row')
Inputs may be any that keep to these rules, and one draw needn't show every extreme that they name: `proj_moments`: index 0 of the leading dimension holds first moments, index 1 second moments, which are positive. `conv_moments`: index 0 of the leading dimension holds first moments, index 1 second moments, which are positive. `mixer_moments`: index 0 of the leading dimension holds first moments, index 1 second moments, which are positive. `up_moments`: index 0 of the leading dimension holds first moments, index 1 second moments, which are positive. `down_moments`: index 0 of the leading dimension holds first moments, index 1 second moments, which are positive. `gains_moments`: index 0 of the leading dimension holds first moments, index 1 second moments, which are positive.
All inputs are finite; a program needn't handle non-finite values.
Results may differ from a plain program's by a relative error of at most 0.012.
The roundings to bfloat16 on the way count: a program that leaves them out, or rounds other values in their place, can miss the bound.
Values may be sent and summed in bfloat16 or wider, within the bound.
A program may use at most 128 MiB of HBM per device.

v0:
```python
import itertools
import math

import jax
import jax.numpy as jnp
from jax import lax
from jax.experimental import pallas as pl
from jax.experimental.pallas import tpu as pltpu
from jax.sharding import PartitionSpec as P

D = 1024
KERNEL = 3
STEP = 4


eps_norm = 1e-05
beta_first = 0.9
beta_second = 0.999
eps_adam = 1e-08
matrix_rate = 0.01
small_rate = 0.1
decay_rate = 0.1


def plain_product(left_side, right_side):
    return jnp.dot(left_side, right_side, preferred_element_type=jnp.float32)


def contract_rows(left_side, right_side):
    return lax.dot_general(
        left_side, right_side, (((0,), (0,)), ((), ())), preferred_element_type=jnp.float32
    )


def contract_cols(left_side, right_side):
    return lax.dot_general(
        left_side, right_side, (((1,), (1,)), ((), ())), preferred_element_type=jnp.float32
    )


def adam_step(parameter, gradient, moments, step_rate, decay_weight):
    first_moment = beta_first * moments[0] + (1.0 - beta_first) * gradient
    second_moment = beta_second * moments[1] + (1.0 - beta_second) * gradient * gradient
    first_hat = first_moment / (1.0 - beta_first**STEP)
    second_hat = second_moment / (1.0 - beta_second**STEP)
    update = first_hat / (jnp.sqrt(second_hat) + eps_adam) + decay_weight * parameter
    is_first = lax.broadcasted_iota(jnp.int32, moments.shape, 0) == 0
    moments_new = jnp.where(
        is_first,
        beta_first * moments + (1.0 - beta_first) * gradient[None],
        beta_second * moments + (1.0 - beta_second) * gradient[None] * gradient[None],
    )
    return (parameter - step_rate * update, moments_new)


def exchange(ids, *items):
    count = len(items)
    groups = []
    for axes, _, _ in items:
        if axes not in groups:
            groups.append(axes)
    sizes = {axes: [lax.axis_size(axis) for axis in axes] for axes in groups}
    devices = {axes: math.prod(sizes[axes]) for axes in groups}
    most = max(devices.values())

    def kernel(*refs):
        sources, targets = refs[:count], refs[count : 2 * count]
        send_sem, recv_sem, own_sem = refs[2 * count :]
        mine, peers = {}, {}
        for axes in groups:
            me = jnp.int32(0)
            for axis, size in zip(axes, sizes[axes]):
                me = me * size + lax.axis_index(axis)
            mine[axes] = me
            peers[axes] = []
            for step in range(1, devices[axes]):
                peer = lax.rem(me + step, devices[axes])
                place, index = {}, peer
                for axis, size in reversed(list(zip(axes, sizes[axes]))):
                    place[axis] = lax.rem(index, size)
                    index = index // size
                peers[axes].append((peer, place))
        barrier = pltpu.get_barrier_semaphore()
        for axes in groups:
            for _, place in peers[axes]:
                pl.semaphore_signal(
                    barrier, inc=1, device_id=place, device_id_type=pl.DeviceIdType.MESH
                )
        pl.semaphore_wait(barrier, sum(len(peers[axes]) for axes in groups))
        copies = []
        for item, (axes, _, whole) in enumerate(items):
            for step, (peer, place) in enumerate(peers[axes]):
                copies.append(
                    pltpu.make_async_remote_copy(
                        src_ref=sources[item] if whole else sources[item].at[peer],
                        dst_ref=targets[item].at[mine[axes]],
                        send_sem=send_sem.at[item, step],
                        recv_sem=recv_sem.at[item, step],
                        device_id=place,
                        device_id_type=pl.DeviceIdType.MESH,
                    )
                )
        for item, (axes, _, whole) in enumerate(items):
            copies.append(
                pltpu.make_async_copy(
                    sources[item] if whole else sources[item].at[mine[axes]],
                    targets[item].at[mine[axes]],
                    own_sem.at[item],
                )
            )
        for copy in copies:
            copy.start()
        for copy in copies:
            copy.wait()

    return pl.pallas_call(
        kernel,
        out_shape=[
            jax.ShapeDtypeStruct(
                (devices[axes],) + tuple(x.shape if whole else x.shape[1:]), x.dtype
            )
            for axes, x, whole in items
        ],
        in_specs=[pl.BlockSpec(memory_space=pl.ANY)] * count,
        out_specs=[pl.BlockSpec(memory_space=pltpu.VMEM)] * count,
        scratch_shapes=[
            pltpu.SemaphoreType.DMA((count, most - 1)),
            pltpu.SemaphoreType.DMA((count, most - 1)),
            pltpu.SemaphoreType.DMA((count,)),
        ],
        compiler_params=pltpu.CompilerParams(collective_id=next(ids), has_side_effects=True),
    )(*[x for _, x, _ in items])


DP, ROW, COL = ("dp",), ("row",), ("col",)


def gather(axes, x):
    return (axes, x, True)


def swap(axes, x):
    blocks = math.prod(lax.axis_size(axis) for axis in axes)
    low = x.astype(jnp.bfloat16)
    return (axes, low.reshape((blocks, -1) + x.shape[1:]), False)


def flat_rows(gathered):
    return gathered.reshape((-1,) + gathered.shape[2:])


def added(blocks):
    total = blocks[0].astype(jnp.float32)
    for index in range(1, blocks.shape[0]):
        total = total + blocks[index].astype(jnp.float32)
    return total


def inverse_rms(row_total):
    return lax.rsqrt(row_total / D + eps_norm)[:, None]


def square_sums(residual):
    return jnp.sum(residual * residual, axis=1)[None, :]


def back_sums(residual, gain_row, d_normed):
    return jnp.sum(d_normed * gain_row * residual, axis=1)[None, :]


def norm_back(residual, inverse, gain_row, d_normed, row_total):
    scaled = d_normed * gain_row
    row_mean = row_total[:, None] / D
    return inverse * (scaled - residual * inverse * inverse * row_mean)


def gain_sums(residual, inverse, d_normed):
    return jnp.sum(d_normed * residual * inverse, axis=0)


def on_device(
    block_input,
    out_cot,
    proj_weight,
    conv_weight,
    mixer_weight,
    up_weight,
    down_weight,
    norm_gains,
    proj_moments,
    conv_moments,
    mixer_moments,
    up_moments,
    down_moments,
    gains_moments,
):
    ids = itertools.count()
    low = jnp.bfloat16
    up_turned = up_weight.transpose(1, 2, 0)
    up_low = up_turned.astype(low)
    stats, wide_proj, conv_wide, wide_mixer, wide_gate, wide_lift, wide_down = exchange(
        ids,
        gather(ROW, square_sums(block_input)),
        gather(DP, proj_weight.astype(low).transpose(1, 0, 2)),
        gather(DP, conv_weight.astype(low)),
        gather(DP, mixer_weight.astype(low)),
        gather(DP, up_low[0]),
        gather(DP, up_low[1]),
        gather(DP, down_weight.astype(low)),
    )
    replicas = wide_proj.shape[0]
    width_local = proj_weight.shape[0]
    shard_width = proj_weight.shape[2]
    channels = replicas * shard_width
    proj_matrix = wide_proj.transpose(2, 1, 0, 3).reshape(width_local, 3 * channels)
    wide_mixer, wide_gate, wide_lift, wide_down = map(
        flat_rows, (wide_mixer, wide_gate, wide_lift, wide_down)
    )
    conv_taps = conv_wide.transpose(1, 0, 2).reshape(KERNEL, channels).astype(jnp.float32)
    gain_one = norm_gains[0]
    gain_two = norm_gains[1]
    history = KERNEL - 1
    inverse_one = inverse_rms(added(stats)[0])
    normed_one = (block_input * inverse_one * gain_one).astype(low)
    gathered_one = flat_rows(exchange(ids, gather(COL, normed_one))[0])
    projected_item = swap(ROW, plain_product(gathered_one, proj_matrix))
    before_blocks = jnp.roll(projected_item[1][:, -history:], 1, axis=0)
    projected, before, gathered_cot = exchange(
        ids,
        projected_item,
        (ROW, before_blocks, False),
        gather(COL, out_cot.astype(low)),
    )
    before = added(before)
    projected = added(projected)
    gathered_cot = flat_rows(gathered_cot)
    inner_rows = projected.shape[0]
    half = wide_down.shape[0] // 256 * 128 or wide_down.shape[0] // 2
    gate_b = projected[:, :channels]
    gate_c = projected[:, channels : 2 * channels]
    values_x = projected[:, 2 * channels :]
    mixed_input = gate_b * values_x
    row_index = lax.axis_index("row")
    before_mixed = before[:, :channels] * before[:, 2 * channels :]
    left_rim = jnp.where(row_index > 0, before_mixed, 0.0)
    padded = jnp.concatenate([left_rim, mixed_input], axis=0)
    convolved = conv_taps[0] * padded[0:inner_rows]
    for offset in range(1, KERNEL):
        convolved = convolved + conv_taps[offset] * padded[offset : offset + inner_rows]
    gated = (gate_c * convolved).astype(low)
    gathered_gated, gate_rims = exchange(ids, gather(ROW, gated), gather(ROW, gate_c[:history]))
    gathered_gated = flat_rows(gathered_gated)
    row_devices = lax.axis_size("row")
    gate_after = lax.dynamic_index_in_dim(
        gate_rims, lax.rem(row_index + 1, row_devices), 0, keepdims=False
    )
    mixer_out, d_hidden_a = exchange(
        ids,
        swap(COL, plain_product(gathered_gated, wide_mixer)),
        swap(ROW, contract_cols(gathered_cot, wide_down[:half])),
    )
    residual_two = block_input + added(mixer_out)
    (stats,) = exchange(ids, gather(ROW, square_sums(residual_two)))
    inverse_two = inverse_rms(added(stats)[0])
    normed_two = (residual_two * inverse_two * gain_two).astype(low)
    gathered_two, d_hidden_b = exchange(
        ids,
        gather(COL, normed_two),
        swap(ROW, contract_cols(gathered_cot, wide_down[half:])),
    )
    gathered_two = flat_rows(gathered_two)
    d_hidden = jnp.concatenate([added(d_hidden_a), added(d_hidden_b)], axis=1)
    gate_pre, lifted = map(
        added,
        exchange(
            ids,
            swap(ROW, contract_cols(gathered_two, wide_gate)),
            swap(ROW, contract_cols(gathered_two, wide_lift)),
        ),
    )
    sigmoid_gate = jax.nn.sigmoid(gate_pre)
    swish_gate = gate_pre * sigmoid_gate
    hidden = (swish_gate * lifted).astype(low)
    d_gate = d_hidden * lifted * sigmoid_gate * (1.0 + gate_pre * (1.0 - sigmoid_gate))
    d_lifted = d_hidden * swish_gate
    d_gate = d_gate.astype(low)
    d_lifted = d_lifted.astype(low)
    unit_sums = jnp.sum(d_gate * gate_pre + d_lifted * lifted, axis=1)[None, :]
    gathered_dgate, gathered_dlift, unit_sums = exchange(
        ids, gather(ROW, d_gate), gather(ROW, d_lifted), gather(ROW, unit_sums)
    )
    gathered_dgate, gathered_dlift = map(flat_rows, (gathered_dgate, gathered_dlift))
    token_sums = unit_sums.reshape(lax.axis_size("col"), 1, -1)
    d_normed_two, hidden_a, token_sums = exchange(
        ids,
        swap(
            COL,
            plain_product(gathered_dgate, wide_gate) + plain_product(gathered_dlift, wide_lift),
        ),
        gather(ROW, hidden[:, :half]),
        (COL, token_sums, False),
    )
    d_normed_two = added(d_normed_two)
    d_residual = out_cot + norm_back(
        residual_two, inverse_two, gain_two, d_normed_two, added(token_sums)[0] / inverse_two[:, 0]
    )
    gathered_dres, hidden_b = exchange(
        ids, gather(COL, d_residual.astype(low)), gather(ROW, hidden[:, half:])
    )
    gathered_dres = flat_rows(gathered_dres)
    hidden_a, hidden_b = map(flat_rows, (hidden_a, hidden_b))
    d_gated_item = swap(ROW, contract_cols(gathered_dres, wide_mixer))
    after_blocks = jnp.roll(d_gated_item[1][:, :history], -1, axis=0)
    d_gated, d_gated_after = map(
        added, exchange(ids, d_gated_item, (ROW, after_blocks, False))
    )
    d_convolved = d_gated * gate_c
    d_gate_c = d_gated * convolved
    next_rim = jnp.where(row_index < row_devices - 1, d_gated_after * gate_after, 0.0)
    extended = jnp.concatenate([d_convolved, next_rim], axis=0)
    d_mixed = conv_taps[history] * extended[0:inner_rows]
    for offset in range(1, KERNEL):
        d_mixed = d_mixed + conv_taps[history - offset] * extended[offset : offset + inner_rows]
    conv_part = jnp.stack(
        [
            jnp.sum(d_convolved * padded[offset : offset + inner_rows], axis=0)
            for offset in range(KERNEL)
        ]
    )
    d_projected = jnp.concatenate([d_mixed * values_x, d_gate_c, d_mixed * gate_b], axis=1).astype(
        low
    )
    gathered_dproj, ffn_out, conv_parts = exchange(
        ids,
        gather(ROW, d_projected),
        swap(
            COL,
            plain_product(hidden_a, wide_down[:half]) + plain_product(hidden_b, wide_down[half:]),
        ),
        gather(("dp", "row"), conv_part),
    )
    gathered_dproj = flat_rows(gathered_dproj)
    block_output = residual_two + added(ffn_out)
    down_part = jnp.concatenate(
        [
            contract_rows(hidden_a, gathered_cot).astype(low),
            contract_rows(hidden_b, gathered_cot).astype(low),
        ],
        axis=0,
    )
    proj_part = contract_rows(gathered_one, gathered_dproj).astype(low)
    proj_part = proj_part.reshape(width_local, 3, replicas, shard_width).transpose(2, 1, 0, 3)
    d_normed_one, proj_grad, mixer_grad, up_grad_gate, up_grad_lift, down_grad = map(
        added,
        exchange(
            ids,
            swap(COL, contract_cols(gathered_dproj, proj_matrix)),
            (DP, proj_part, False),
            swap(DP, contract_rows(gathered_gated, gathered_dres)),
            swap(DP, contract_rows(gathered_dgate, gathered_two)),
            swap(DP, contract_rows(gathered_dlift, gathered_two)),
            swap(DP, down_part),
        ),
    )
    gains_part = jnp.stack(
        [
            gain_sums(block_input, inverse_one, d_normed_one),
            gain_sums(residual_two, inverse_two, d_normed_two),
        ]
    )
    stats, gains_parts = exchange(
        ids,
        gather(ROW, back_sums(block_input, gain_one, d_normed_one)),
        gather(("dp", "col"), gains_part),
    )
    input_grad = d_residual + norm_back(
        block_input, inverse_one, gain_one, d_normed_one, added(stats)[0]
    )
    proj_grad = proj_grad.transpose(1, 0, 2)
    up_grad = jnp.stack([up_grad_gate, up_grad_lift]).transpose(2, 0, 1)
    conv_grad = lax.dynamic_slice_in_dim(
        added(conv_parts), lax.axis_index("dp") * shard_width, shard_width, 1
    )
    gains_grad = added(gains_parts)
    proj_new, proj_moments_new = adam_step(
        proj_weight, proj_grad, proj_moments, matrix_rate, decay_rate
    )
    conv_new, conv_moments_new = adam_step(conv_weight, conv_grad, conv_moments, small_rate, 0.0)
    mixer_new, mixer_moments_new = adam_step(
        mixer_weight, mixer_grad, mixer_moments, matrix_rate, decay_rate
    )
    up_new, up_moments_new = adam_step(up_weight, up_grad, up_moments, matrix_rate, decay_rate)
    down_new, down_moments_new = adam_step(
        down_weight, down_grad, down_moments, matrix_rate, decay_rate
    )
    gains_new, gains_moments_new = adam_step(norm_gains, gains_grad, gains_moments, small_rate, 0.0)
    return (
        block_output,
        input_grad,
        proj_grad,
        conv_grad,
        mixer_grad,
        up_grad,
        down_grad,
        gains_grad,
        proj_new,
        conv_new,
        mixer_new,
        up_new,
        down_new,
        gains_new,
        proj_moments_new,
        conv_moments_new,
        mixer_moments_new,
        up_moments_new,
        down_moments_new,
        gains_moments_new,
    )


def solution(mesh):
    in_specs = (
        P(("dp", "col"), "row"),
        P(("dp", "col"), "row"),
        P("row", None, ("dp", "col")),
        P(None, ("dp", "col")),
        P(("dp", "col"), "row"),
        P("row", None, ("dp", "col")),
        P(("dp", "col"), "row"),
        P(None, "row"),
        P(None, "row", None, ("dp", "col")),
        P(None, None, ("dp", "col")),
        P(None, ("dp", "col"), "row"),
        P(None, "row", None, ("dp", "col")),
        P(None, ("dp", "col"), "row"),
        P(None, None, "row"),
    )
    out_specs = (
        P(("dp", "col"), "row"),
        P(("dp", "col"), "row"),
        P("row", None, ("dp", "col")),
        P(None, ("dp", "col")),
        P(("dp", "col"), "row"),
        P("row", None, ("dp", "col")),
        P(("dp", "col"), "row"),
        P(None, "row"),
        P("row", None, ("dp", "col")),
        P(None, ("dp", "col")),
        P(("dp", "col"), "row"),
        P("row", None, ("dp", "col")),
        P(("dp", "col"), "row"),
        P(None, "row"),
        P(None, "row", None, ("dp", "col")),
        P(None, None, ("dp", "col")),
        P(None, ("dp", "col"), "row"),
        P(None, "row", None, ("dp", "col")),
        P(None, ("dp", "col"), "row"),
        P(None, None, "row"),
    )
    return jax.shard_map(
        on_device, mesh=mesh, in_specs=in_specs, out_specs=out_specs, check_vma=False
    )
```

profile of v0, /device:TPU:0, one launch (start us, length us, event | category | flops | bytes accessed | tf_op | source)
XLA Modules:
  0.0 256.6 jit_solution(7116183977674964111)
XLA Ops:
  0.7 1.4 convert_bitcast_fusion
  6.3 8.4 %shard_map.293 = (f32[4,1,128]{2,1,0:T(1,128)}, bf16[2,3,256,128]{3,2,1,0:T(8,128)(2,1)}, bf16[2,3,128]{2,1,0:T(4,128)(2,1)}, bf16[2,128,256]{2,1,0:T(8,128)(2,1...) custom-call(f32[1,128]{1,0:T(1,128)} %bitcast.409, ...), custom_call_target="tpu_custom_call" | custom-call | tf_op jit(solution)/shard_map/pallas_call | solution.py:116
  16.1 10.2 %shard_map.294 = bf16[4,128,256]{2,1,0:T(8,128)(2,1)} custom-call(bf16[128,256]{1,0:T(8,128)(2,1)} %multiply_convert_fusion.5.refs_0_), custom_call_target="tpu_custom_call" | custom-call | tf_op jit(solution)/shard_map/pallas_call | solution.py:116
  26.3 1.2 copy.42
  27.5 1.4 convolution_convert_fusion.2
  30.3 13.5 %shard_map.295 = (bf16[4,128,768]{2,1,0:T(8,128)(2,1)}, bf16[4,2,768]{2,1,0:T(2,128)(2,1)}, bf16[4,128,256]{2,1,0:T(8,128)(2,1)}) custom-call(bf16[4,128,768]{2,1,0:T(8,128)(2,1)} %bitcast.353, bf16[4,2,768]{2,1,0:T(2,128)(2,1)} %pad_maximum_fusion.5.refs_1_, bf16[128,256]{1,0:T(8,128)(2,1)} %convert_element_type.352.refs_2_), custom_call_target="tpu_custom_call" | custom-call | tf_op jit(solution)/shard_map/pallas_call | solution.py:116
  43.9 1.4 add_bitcast_fusion.1
  46.7 7.4 %shard_map.296 = (bf16[4,128,256]{2,1,0:T(8,128)(2,1)}, f32[4,2,256]{2,1,0:T(2,128)}) custom-call(bf16[128,256]{1,0:T(8,128)(2,1)} %get-tuple-element.129.refs_0_, f32[2,256]{1,0:T(2,128)} %slice.543.refs_1_), custom_call_target="tpu_custom_call" | custom-call | tf_op jit(solution)/shard_map/pallas_call | solution.py:116
  54.2 1.9 convolution_convert_fusion.7
  56.0 1.1 convolution_convert_fusion.4
  57.2 9.3 %shard_map.297 = (bf16[4,128,256]{2,1,0:T(8,128)(2,1)}, bf16[4,128,512]{2,1,0:T(8,128)(2,1)}) custom-call(bf16[4,128,256]{2,1,0:T(8,128)(2,1)} %bitcast.376, bf16[4,128,512]{2,1,0:T(8,128)(2,1)} %bitcast.366), custom_call_target="tpu_custom_call" | custom-call | tf_op jit(solution)/shard_map/pallas_call | solution.py:116
  66.4 1.6 multiply_reduce_fusion.4
  68.0 5.9 %shard_map.298 = f32[4,1,128]{2,1,0:T(1,128)} custom-call(f32[1,128]{1,0:T(1,128)} %bitcast.411), custom_call_target="tpu_custom_call" | custom-call | tf_op jit(solution)/shard_map/pallas_call | solution.py:116
  75.3 1.2 convolution_convert_fusion.3
  76.5 10.4 %shard_map.299 = (bf16[4,128,256]{2,1,0:T(8,128)(2,1)}, bf16[4,128,640]{2,1,0:T(8,128)(2,1)}) custom-call(bf16[128,256]{1,0:T(8,128)(2,1)} %multiply_convert_fusion.3.refs_0_, bf16[4,128,640]{2,1,0:T(8,128)(2,1)} %bitcast.355), custom_call_target="tpu_custom_call" | custom-call | tf_op jit(solution)/shard_map/pallas_call | solution.py:116
  86.9 2.6 %convolution_convert_fusion = bf16[512,1152]{1,0:T(8,128)(2,1)} fusion(bf16[512,256]{1,0:T(8,128)(2,1)} %bitcast.382, bf16[1152,256]{1,0:T(8,128)(2,1)S(1)} %bitcast.361), kind=kOutput, calls=%fused_computation | convolution fusion | flops 302579712 | bytes 2031616 | tf_op jit(solution)/shard_map/dot_general | solution.py:36
  89.5 1.6 convolution_convert_fusion.1
  91.1 27.7 %shard_map.300 = (bf16[4,128,1152]{2,1,0:T(8,128)(2,1)}, bf16[4,128,1152]{2,1,0:T(8,128)(2,1)}) custom-call(bf16[4,128,1152]{2,1,0:T(8,128)(2,1)} %bitcast.348, bf16[4,128,1152]{2,1,0:T(8,128)(2,1)} %bitcast.347), custom_call_target="tpu_custom_call" | custom-call | tf_op jit(solution)/shard_map/pallas_call | solution.py:116
  118.8 2.1 fusion.33
  121.1 1.1 copy-done.2
  122.2 1.8 fusion.31
  124.0 29.4 %shard_map.301 = (bf16[4,128,1152]{2,1,0:T(8,128)(2,1)}, bf16[4,128,1152]{2,1,0:T(8,128)(2,1)}, f32[4,1,128]{2,1,0:T(1,128)}) custom-call(bf16[128,1152]{1,0:T(8,128)(2,1)} %get-tuple-element.124.refs_0_, bf16[128,1152]{1,0:T(8,128)(2,1)} %get-tuple-element.123.refs_1_, f32[1,128]{1,0:T(1,128)} %bitcast.412), custom_call_target="tpu_custom_call" | custom-call | tf_op jit(solution)/shard_map/pallas_call | solution.py:116
  153.4 1.9 fusion.98
  155.3 1.2 fusion.4
  157.2 9.8 %shard_map.302 = (bf16[4,128,256]{2,1,0:T(8,128)(2,1)}, bf16[4,128,512]{2,1,0:T(8,128)(2,1)}, f32[4,1,128]{2,1,0:T(1,128)}) custom-call(bf16[4,128,256]{2,1,0:T(8,128)(2,1)} %bitcast.375, bf16[128,512]{1,0:T(8,128)(2,1)} %slice.546.refs_1_, f32[4,1,128]{2,1,0:T(1,128)} %get-tuple-element.78.refs_2_), custom_call_target="tpu_custom_call" | custom-call | tf_op jit(solution)/shard_map/pallas_call | solution.py:116
  167.6 1.7 fusion.92
  170.1 9.5 %shard_map.303 = (bf16[4,128,256]{2,1,0:T(8,128)(2,1)}, bf16[4,128,640]{2,1,0:T(8,128)(2,1)}) custom-call(bf16[128,256]{1,0:T(8,128)(2,1)} %get-tuple-element.118.refs_0_, bf16[128,640]{1,0:T(8,128)(2,1)} %slice.547.refs_1_), custom_call_target="tpu_custom_call" | custom-call | tf_op jit(solution)/shard_map/pallas_call | solution.py:116
  179.6 1.5 fusion.3
  182.4 1.3 fusion.1
  183.8 1.3 fusion
  187.0 6.9 %shard_map.304 = (bf16[4,128,256]{2,1,0:T(8,128)(2,1)}, bf16[4,2,256]{2,1,0:T(2,128)(2,1)}) custom-call(bf16[4,128,256]{2,1,0:T(8,128)(2,1)} %bitcast.373, bf16[4,2,256]{2,1,0:T(2,128)(2,1)} %pad_maximum_fusion.6.refs_1_), custom_call_target="tpu_custom_call" | custom-call | tf_op jit(solution)/shard_map/pallas_call | solution.py:116
  194.0 1.0 multiply_reduce_fusion.3
  195.6 1.3 fusion.45
  197.0 1.1 fusion.5
  199.6 14.3 %shard_map.305 = (bf16[4,128,768]{2,1,0:T(8,128)(2,1)}, bf16[4,128,256]{2,1,0:T(8,128)(2,1)}, f32[8,3,256]{2,1,0:T(4,128)}) custom-call(bf16[128,768]{1,0:T(8,128)(2,1)} %pad_maximum_fusion.2.refs_0_, bf16[4,128,256]{2,1,0:T(8,128)(2,1)} %bitcast.374, f32[3,256]{1,0:T(4,128)} %pad_maximum_fusion.7.refs_2_), custom_call_target="tpu_custom_call" | custom-call | tf_op jit(solution)/shard_map/pallas_call | solution.py:116
  213.9 1.6 fusion.2
  216.6 1.1 convolution_convert_fusion.5
  217.7 10.5 %shard_map.306 = (bf16[4,128,256]{2,1,0:T(8,128)(2,1)}, bf16[2,3,256,128]{3,2,1,0:T(8,128)(2,1)}, bf16[2,128,256]{2,1,0:T(8,128)(2,1)}, bf16[2,576,256]{2,1,0:T(...) custom-call(bf16[4,128,256]{2,1,0:T(8,128)(2,1)} %bitcast.381, ...), custom_call_target="tpu_custom_call" | custom-call | tf_op jit(solution)/shard_map/pallas_call | solution.py:116
  228.2 2.4 fusion.63
  231.2 7.0 %shard_map.307 = (f32[4,1,128]{2,1,0:T(1,128)}, f32[8,2,256]{2,1,0:T(2,128)}) custom-call(f32[1,128]{1,0:T(1,128)} %bitcast.410, f32[2,256]{1,0:T(2,128)} %pad_maximum_fusion.8.refs_1_), custom_call_target="tpu_custom_call" | custom-call | tf_op jit(solution)/shard_map/pallas_call | solution.py:116
  239.8 1.3 add_select_fusion.1
  241.6 1.9 copy-done
  243.8 1.9 multiply_multiply_fusion
  245.7 1.8 add_select_fusion
  249.7 1.1 broadcast_multiply_fusion.1
  250.8 1.1 multiply_multiply_fusion.3
  251.9 1.1 add_select_fusion.2
  253.0 1.5 multiply_subtract_fusion
  (176 shorter events, 25.5 us)
Async XLA Ops:
  0.7 2.3 copy-start.10
  2.1 1.6 copy-start.16
  2.1 2.3 copy-start.45
  2.1 3.0 %copy-start.55 = (f32[3,128]{1,0:T(4,128)S(1)}, f32[3,128]{1,0:T(4,128)}, u32[]{:S(2)}) copy-start(f32[3,128]{1,0:T(4,128)} %param.17) | copy-start | bytes 4612
  2.1 3.5 %copy-start.5 = (f32[128,256]{1,0:T(8,128)S(1)}, f32[128,256]{1,0:T(8,128)}, u32[]{:S(2)}) copy-start(f32[128,256]{1,0:T(8,128)} %param.14) | copy-start | bytes 393220
  3.7 11.6 %copy-start.53 = (f32[2,256]{1,0:T(2,128)S(1)}, f32[2,256]{1,0:T(2,128)}, u32[]{:S(2)}) copy-start(f32[2,256]{1,0:T(2,128)} %param.21) | copy-start | bytes 6148
  26.3 3.4 %copy-start.42 = (f32[128,256]{1,0:T(8,128)S(1)}, f32[128,256]{1,0:T(8,128)}, u32[]{:S(2)}) copy-start(f32[128,256]{1,0:T(8,128)} %param.15) | copy-start | bytes 393220
  28.9 1.4 copy-start.6
  30.3 15.0 %copy-start.57 = (bf16[2,3,128]{2,1,0:T(4,128)(2,1)S(1)}, bf16[2,3,128]{2,1,0:T(4,128)(2,1)}, u32[]{:S(2)}) copy-start(bf16[2,3,128]{2,1,0:T(4,128)(2,1)} %get-tuple-element.62) | copy-start | bytes 4612
  43.8 1.5 copy-start.51
  43.8 10.3 %copy-start.36 = (bf16[2,128,256]{2,1,0:T(8,128)(2,1)S(1)}, bf16[2,128,256]{2,1,0:T(8,128)(2,1)}, u32[]{:S(2)}) copy-start(bf16[2,128,256]{2,1,0:T(8,128)(2,1)} %get-tuple-element.65) | copy-start | bytes 393220
  43.8 12.2 %copy-start.12 = (bf16[2,576,256]{2,1,0:T(8,128)(2,1)S(1)}, bf16[2,576,256]{2,1,0:T(8,128)(2,1)}, u32[]{:S(2)}) copy-start(bf16[2,576,256]{2,1,0:T(8,128)(2,1)} %get-tuple-element.67) | copy-start | bytes 1769476
  43.8 12.2 %copy-start.24 = (bf16[4,128,256]{2,1,0:T(8,128)(2,1)S(1)}, bf16[4,128,256]{2,1,0:T(8,128)(2,1)}, u32[]{:S(2)}) copy-start(bf16[4,128,256]{2,1,0:T(8,128)(2,1)} %get-tuple-element.66) | copy-start | bytes 786436
  45.3 21.2 %copy-start.20 = (f32[128,256]{1,0:T(8,128)}, f32[128,256]{1,0:T(8,128)S(1)}, u32[]{:S(2)}) copy-start(f32[128,256]{1,0:T(8,128)S(1)} %slice_multiply_fusion) | copy-start | bytes 393220
  68.0 18.9 %copy-start.13 = (bf16[2,576,256]{2,1,0:T(8,128)(2,1)S(1)}, bf16[2,576,256]{2,1,0:T(8,128)(2,1)}, u32[]{:S(2)}) copy-start(bf16[2,576,256]{2,1,0:T(8,128)(2,1)} %get-tuple-element.73) | copy-start | bytes 1769476
  86.9 2.6 %copy-start.14 = (bf16[2,576,256]{2,1,0:T(8,128)(2,1)S(1)}, bf16[2,576,256]{2,1,0:T(8,128)(2,1)}, u32[]{:S(2)}) copy-start(bf16[2,576,256]{2,1,0:T(8,128)(2,1)} %get-tuple-element.72) | copy-start | bytes 1769476
  86.9 2.6 %copy-start.30 = (bf16[4,128,256]{2,1,0:T(8,128)(2,1)S(1)}, bf16[4,128,256]{2,1,0:T(8,128)(2,1)}, u32[]{:S(2)}) copy-start(bf16[4,128,256]{2,1,0:T(8,128)(2,1)} %get-tuple-element.71) | copy-start | bytes 786436
  118.8 2.1 copy-start.33
  118.8 2.2 copy-start.38
  153.4 1.9 copy-start.18
  155.3 12.4 %copy-start.43 = (f32[128,256]{1,0:T(8,128)S(1)}, f32[128,256]{1,0:T(8,128)}, u32[]{:S(2)}) copy-start(f32[128,256]{1,0:T(8,128)} %param.15) | copy-start | bytes 393220
  156.5 23.1 %copy-start.25 = (bf16[4,128,256]{2,1,0:T(8,128)(2,1)S(1)}, bf16[4,128,256]{2,1,0:T(8,128)(2,1)}, u32[]{:S(2)}) copy-start(bf16[4,128,256]{2,1,0:T(8,128)(2,1)} %get-tuple-element.66) | copy-start | bytes 786436
  169.4 11.7 %copy-start.39 = (bf16[4,128,512]{2,1,0:T(8,128)(2,1)S(1)}, bf16[4,128,512]{2,1,0:T(8,128)(2,1)}, u32[]{:S(2)}) copy-start(bf16[4,128,512]{2,1,0:T(8,128)(2,1)} %get-tuple-element.85) | copy-start | bytes 1572868
  183.8 1.4 copy-start.26
  183.8 1.4 copy-start.27
  183.8 2.3 copy-start.37
  185.1 8.9 %copy-start.21 = (f32[128,256]{1,0:T(8,128)S(1)}, f32[128,256]{1,0:T(8,128)}, u32[]{:S(2)}) copy-start(f32[128,256]{1,0:T(8,128)} %copy-done.20) | copy-start | bytes 393220
  185.1 8.9 %copy-start.41 = (f32[128,256]{1,0:T(8,128)S(1)}, f32[128,256]{1,0:T(8,128)}, u32[]{:S(2)}) copy-start(f32[128,256]{1,0:T(8,128)} %get-tuple-element.130) | copy-start | bytes 393220
  187.0 10.0 %copy-start.32 = (bf16[4,128,640]{2,1,0:T(8,128)(2,1)S(1)}, bf16[4,128,640]{2,1,0:T(8,128)(2,1)}, u32[]{:S(2)}) copy-start(bf16[4,128,640]{2,1,0:T(8,128)(2,1)} %get-tuple-element.86) | copy-start | bytes 1966084
  198.1 15.8 %copy-start.15 = (bf16[4,128,256]{2,1,0:T(8,128)(2,1)S(1)}, bf16[4,128,256]{2,1,0:T(8,128)(2,1)}, u32[]{:S(2)}) copy-start(bf16[4,128,256]{2,1,0:T(8,128)(2,1)} %shard_map.294) | copy-start | bytes 786436
  213.9 2.7 %copy-start.8 = (bf16[4,128,768]{2,1,0:T(8,128)(2,1)S(1)}, bf16[4,128,768]{2,1,0:T(8,128)(2,1)}, u32[]{:S(2)}) copy-start(bf16[4,128,768]{2,1,0:T(8,128)(2,1)} %get-tuple-element.88) | copy-start | bytes 2359300
  217.7 10.5 %copy-start.29 = (f32[2,128,256]{2,1,0:T(8,128)S(1)}, f32[2,128,256]{2,1,0:T(8,128)}, u32[]{:S(2)}) copy-start(f32[2,128,256]{2,1,0:T(8,128)} %param.24) | copy-start | bytes 786436
  217.7 10.5 %copy-start.46 = (f32[128,256]{1,0:T(8,128)S(1)}, f32[128,256]{1,0:T(8,128)}, u32[]{:S(2)}) copy-start(f32[128,256]{1,0:T(8,128)} %param.18) | copy-start | bytes 393220
  228.2 10.8 %copy-start.50 = (f32[2,2,256]{2,1,0:T(2,128)S(1)}, f32[2,2,256]{2,1,0:T(2,128)}, u32[]{:S(2)}) copy-start(f32[2,2,256]{2,1,0:T(2,128)} %param.27) | copy-start | bytes 12292
  228.2 11.5 %copy-start.9 = (bf16[2,576,256]{2,1,0:T(8,128)(2,1)S(1)}, bf16[2,576,256]{2,1,0:T(8,128)(2,1)}, u32[]{:S(2)}) copy-start(bf16[2,576,256]{2,1,0:T(8,128)(2,1)} %get-tuple-element.96) | copy-start | bytes 1769476
  230.6 9.2 %copy-start.4 = (f32[2,576,256]{2,1,0:T(8,128)S(1)}, f32[2,576,256]{2,1,0:T(8,128)}, u32[]{:S(2)}) copy-start(f32[2,576,256]{2,1,0:T(8,128)} %param.26) | copy-start | bytes 3538948
  239.0 16.3 %copy-start.49 = (f32[1,2,256]{2,1,0:T(2,128)}, f32[1,2,256]{2,1,0:T(2,128)S(1)}, u32[]{:S(2)}) copy-start(f32[1,2,256]{2,1,0:T(2,128)S(1)} %get-tuple-element.104) | copy-start | bytes 6148
  239.8 1.4 copy-start.35
  241.4 2.1 copy-start
  241.4 2.4 copy-start.3
  241.6 4.1 %copy-start.1 = (f32[256,2,576]{0,2,1:T(8,128)}, f32[256,2,576]{0,2,1:T(8,128)S(1)}, u32[]{:S(2)}) copy-start(f32[256,2,576]{0,2,1:T(8,128)S(1)} %get-tuple-element.106) | copy-start | bytes 3538948
  245.7 1.8 copy-start.44
  247.6 3.3 %copy-start.7 = (f32[2,256,3,128]{3,1,2,0:T(8,128)S(1)}, f32[2,256,3,128]{3,1,2,0:T(8,128)}, u32[]{:S(2)}) copy-start(f32[2,256,3,128]{3,1,2,0:T(8,128)} %param.22) | copy-start | bytes 2359300
  248.5 3.4 %copy-start.54 = (f32[3,128]{1,0:T(4,128)}, f32[3,128]{1,0:T(4,128)S(1)}, u32[]{:S(2)}) copy-start(f32[3,128]{1,0:T(4,128)S(1)} %get-tuple-element.108) | copy-start | bytes 4612
  253.0 1.5 copy-start.58
  253.0 1.5 copy-start.28
  253.0 1.5 copy-start.40
  253.0 2.9 %copy-start.47 = (bf16[4,128,256]{2,1,0:T(8,128)(2,1)S(1)}, bf16[4,128,256]{2,1,0:T(8,128)(2,1)}, u32[]{:S(2)}) copy-start(bf16[4,128,256]{2,1,0:T(8,128)(2,1)} %get-tuple-element.87) | copy-start | bytes 786436
  (11 other events, 12.2 us)
where the time goes:
time: 257 us
  Pallas kernels  180 us (70%)
  other arithmetic  42.3 us (16%)
  matrix products  23.6 us (9%)
  local copies, waits for them, and re-layouts  8.95 us (3%)
    pallas_call x15, Pallas kernels, exchange(): pl.pallas_call(kernel, out_shape=[jax.ShapeDtypeStruct((devices[axes],) +...  180 us
    dot_general x6, matrix products, plain_product(): return jnp.dot(left_side, right_side, preferred_element_type=jnp.float32)  8.74 us
    dot_general x6, matrix products, contract_cols(): lax.dot_general(left_side, right_side, (((1,), (1,)), ((), ())), preferre...  7.82 us
    dot_general x6, matrix products, contract_rows(): lax.dot_general(left_side, right_side, (((0,), (0,)), ((), ())), preferre...  7.01 us
    select_n x6, other arithmetic, adam_step(): jnp.where(is_first, beta_first * moments + (1.0 - beta_first) * gradient[...  6.25 us

commit v1 on v0

v1 whole, which is shorter than its diff:
```python
import jax
import jax.numpy as jnp
from jax import lax
from jax.experimental import pallas as pl
from jax.experimental.pallas import tpu as pltpu
from jax.sharding import PartitionSpec as P

KERNEL = 3
STEP = 4
HISTORY = KERNEL - 1
RIM = 8

eps_norm = 1e-05
beta_first = 0.9
beta_second = 0.999
eps_adam = 1e-08
matrix_rate = 0.01
small_rate = 0.1
decay_rate = 0.1

LOW = jnp.bfloat16
F32 = jnp.float32
MESH = pl.DeviceIdType.MESH
VMEM_LIMIT = 60 * 1024 * 1024


def plain_product(left_side, right_side):
    return jnp.dot(left_side, right_side, preferred_element_type=F32)


def contract_rows(left_side, right_side):
    return lax.dot_general(
        left_side, right_side, (((0,), (0,)), ((), ())), preferred_element_type=F32
    )


def contract_cols(left_side, right_side):
    return lax.dot_general(
        left_side, right_side, (((1,), (1,)), ((), ())), preferred_element_type=F32
    )


def adam(parameter, gradient, first, second, step_rate, decay_weight):
    first_moment = beta_first * first + (1.0 - beta_first) * gradient
    second_moment = beta_second * second + (1.0 - beta_second) * gradient * gradient
    first_hat = first_moment / (1.0 - beta_first**STEP)
    second_hat = second_moment / (1.0 - beta_second**STEP)
    update = first_hat / (jnp.sqrt(second_hat) + eps_adam) + decay_weight * parameter
    return parameter - step_rate * update, first_moment, second_moment


def padded_rows(count):
    return -(-count // 16) * 16


class Names:
    def __init__(self, **items):
        self.items = items
        self.__dict__.update(items)

    def bound(self, refs):
        return Names(**dict(zip(self.items, refs)))


class Ring:
    def __init__(self, axis, size):
        assert size & (size - 1) == 0
        self.axis, self.size = axis, size
        self.me = lax.axis_index(axis)

    def peer(self, step):
        index, bit = jnp.int32(0), 1
        while bit < self.size:
            digit = lax.rem(lax.div(self.me, jnp.int32(bit)), jnp.int32(2))
            index = index + ((1 - digit) if step & bit else digit) * bit
            bit *= 2
        return index

    def steps(self):
        return range(1, self.size)


class Shapes:
    def __init__(self, sizes, tokens, width, channels, units):
        self.dp, self.row, self.col = sizes
        self.tokens, self.width = tokens, width
        self.rows = tokens // self.row
        self.length = tokens * self.col
        self.full = width * self.row
        self.stored_chan, self.stored_unit = channels, units
        self.cut_chan, self.cut_unit = channels // self.row, units // self.row
        self.chan = padded_rows(self.cut_chan)
        self.unit = padded_rows(self.cut_unit)
        self.chans = self.chan * self.dp
        self.units = self.unit * self.dp
        self.spots = 8 * (self.col * self.row + self.col) + 20 * self.row + 12 * self.dp + self.col


def block_kernel(s, ins, outs, tmp, send_sem, recv_sem, own_sem):
    dp, row, col = Ring("dp", s.dp), Ring("row", s.row), Ring("col", s.col)
    h, r, c = dp.me, row.me, col.me
    taken = [0]
    sent = []

    barrier = pltpu.get_barrier_semaphore()
    for ring in (row, col, dp):
        for step in ring.steps():
            pl.semaphore_signal(
                barrier, inc=1, device_id={ring.axis: ring.peer(step)}, device_id_type=MESH
            )

    here = ins.bound(tmp.arguments)
    loads = Names(
        **{
            key: pltpu.make_async_copy(source, target, own_sem.at[4 + index])
            for index, (key, source, target) in enumerate(
                zip(ins.items, ins.items.values(), tmp.arguments)
            )
        }
    )
    for copy in loads.items.values():
        copy.start()
    ins = here

    def take(count):
        taken[0] += count
        assert taken[0] <= s.spots
        return taken[0] - count

    def make(src, dst, send, recv, ring, peer):
        return pltpu.make_async_remote_copy(
            src_ref=src,
            dst_ref=dst,
            send_sem=send_sem.at[send],
            recv_sem=recv_sem.at[recv],
            device_id={ring.axis: peer},
            device_id_type=MESH,
        )

    def remote(src, dst, spot, ring, peer):
        copy = make(src, dst, spot, spot, ring, peer)
        copy.start()
        sent.append(copy)
        return copy

    def wait_all(copies):
        for copy in copies:
            copy.wait_recv()

    def span(index, size):
        return pl.ds(pl.multiple_of(index * size, size), size)

    def row_cols(index):
        return span(index, s.width)

    def block(b):
        return pl.ds(b * s.tokens, s.tokens)

    blocks = range(s.col)

    def line(b):
        return pl.ds(pl.multiple_of(b * s.tokens + r * s.rows, s.rows), s.rows)

    class Gather:
        def __init__(self, array, square):
            self.array, self.square = array, square
            self.z, self.xy = take(s.col), take(s.col * s.row)

        def piece(self, b):
            if self.square:
                return self.array.at[span(b, s.tokens), row_cols(r)]
            return self.array.at[line(b), :]

        def z_copy(self, source, target):
            part = self.piece(source)
            return make(part, part, self.z + target, self.z + source, col, target)

        def xy_copy(self, b, other):
            part = self.piece(b)
            spot = self.xy + b * s.row + other
            return make(part, part, spot, spot, row, row.peer(other))

        def start(self, b):
            @pl.when(c == b)
            def _():
                for target in blocks:
                    if target != b:
                        self.z_copy(b, target).start()
                for other in row.steps():
                    self.xy_copy(b, other).start()

        def forward(self, b):
            @pl.when(c != b)
            def _():
                self.z_copy(b, (b + 1) % s.col).wait_recv()
                for other in row.steps():
                    self.xy_copy(b, other).start()

        def wait(self, b):
            for other in row.steps():
                self.xy_copy(b, other).wait_recv()

        def finish(self):
            for b in blocks:
                for other in row.steps():
                    self.xy_copy(b, other).wait_send()

                @pl.when(c == b)
                def _(b=b):
                    for target in blocks:
                        if target != b:
                            self.z_copy(b, target).wait_send()

    class Scatter:
        def __init__(self, out, one, mid, two):
            self.out, self.one, self.mid, self.two = out, one, mid, two
            self.z, self.xy = take(s.col), take(s.col * s.row)

        def xy_copy(self, b, other):
            peer = row.peer(other)
            spot = self.xy + b * s.row + other
            return make(
                self.out.at[b, span(peer, s.rows), :], self.one.at[b, other], spot, spot, row, peer
            )

        def z_copy(self, b, source):
            return make(
                self.mid.at[b], self.two.at[source], self.z + b, self.z + source, col, b
            )

        def chunk(self, b, partial):
            self.out[b] = partial.astype(LOW)
            for other in row.steps():
                self.xy_copy(b, other).start()

        def square_sum(self, b):
            total = self.out[b, span(r, s.rows), :].astype(F32)
            for other in row.steps():
                self.xy_copy(b, other).wait_recv()
                total = total + self.one[b, other].astype(F32)
            return total

        def relay(self, b):
            @pl.when(c != b)
            def _():
                self.mid[b] = self.square_sum(b).astype(LOW)
                self.z_copy(b, c).start()

        def total(self, b):
            total = self.square_sum(b)
            for source in blocks:
                if source != b:
                    self.z_copy(b, source).wait_recv()
                    total = total + self.two[source].astype(F32)
            return total

        def finish(self):
            for b in blocks:
                for other in row.steps():
                    self.xy_copy(b, other).wait_send()

                @pl.when(c != b)
                def _(b=b):
                    self.z_copy(b, c).wait_send()

    def cut(target, values, stored, kept, padded):
        for part in range(s.row):
            lead = (slice(None),) * (len(target.shape) - 3)
            where = lead + (part,) if lead else (part,)
            if padded != kept:
                target[where + (slice(None), slice(None))] = jnp.zeros(
                    target.shape[: len(lead)] + target.shape[-2:], LOW
                )
            piece = values(part * kept, kept)
            target[where + (pl.ds(0, kept), slice(None))] = piece.astype(LOW)

    loads.proj.wait()
    for part in range(3):
        tmp.turned[part] = ins.proj[part].T
    cut(
        tmp.s_proj, lambda at, size: tmp.turned[:, at : at + size, :], 0, s.cut_chan, s.chan
    )
    loads.mixer.wait()
    cut(tmp.s_mixer, lambda at, size: ins.mixer[at : at + size, :], 0, s.cut_chan, s.chan)
    loads.up.wait()
    cut(tmp.s_up, lambda at, size: ins.up[:, at : at + size, :], 0, s.cut_unit, s.unit)
    loads.down.wait()
    cut(tmp.s_down, lambda at, size: ins.down[at : at + size, :], 0, s.cut_unit, s.unit)

    loads.x.wait()
    loads.cot.wait()
    loads.gains.wait()
    loads.taps.wait()
    tmp.x_all[span(c, s.tokens), row_cols(r)] = ins.x[...].astype(LOW)
    tmp.cot_all[span(c, s.tokens), row_cols(r)] = ins.cot[...].astype(LOW)
    tmp.gains_own[...] = jnp.zeros(tmp.gains_own.shape, F32)
    tmp.gains_own[0:2, :] = ins.gains[...]
    tmp.gains_all[:, row_cols(r)] = tmp.gains_own[...]

    def chooser(shape, stored_dim):
        here_dim = 1 - stored_dim
        stored = lax.broadcasted_iota(jnp.int32, shape, stored_dim) - r * s.cut_chan
        here = lax.broadcasted_iota(jnp.int32, shape, here_dim) - h * s.chan
        return ((stored == here) & (here >= 0) & (here < s.cut_chan)).astype(F32)

    stored_taps = jnp.concatenate(
        [ins.taps[...], jnp.zeros((8 - KERNEL, s.stored_chan), F32)], axis=0
    )
    taps = plain_product(
        stored_taps.astype(LOW), chooser((s.stored_chan, s.chans), 0).astype(LOW)
    )
    tmp.tap_own[...] = taps

    pl.semaphore_wait(barrier, s.row + s.col + s.dp - 3)

    own_copies = []

    class Weight:
        def __init__(self, source, target):
            self.lead = (slice(None),) * (len(target.shape) - 2)
            self.size = source.shape[-2]
            self.target = target
            self.spot, self.across = take(s.row), take(s.dp)
            view = target.at[self.lead + (span(h, self.size), row_cols(r))]
            self.copies = [
                remote(
                    source.at[self.lead + (row.peer(other),)],
                    view,
                    self.spot + other,
                    row,
                    row.peer(other),
                )
                for other in row.steps()
            ]
            self.own = pltpu.make_async_copy(
                source.at[self.lead + (r,)], view, own_sem.at[len(own_copies)]
            )
            self.own.start()
            own_copies.append(self.own)

        def forward(self):
            wait_all(self.copies)
            self.own.wait()
            view = self.target.at[self.lead + (span(h, self.size), slice(None))]
            self.across_copies = [
                remote(view, view, self.across + step, dp, dp.peer(step)) for step in dp.steps()
            ]

        def wait(self):
            wait_all(self.across_copies)

    class Gradient:
        def __init__(self, whole, low, land, mine, out):
            self.whole, self.low, self.land, self.mine, self.out = whole, low, land, mine, out
            self.lead = (slice(None),) * (len(whole.shape) - 2)
            self.size = whole.shape[-2] // s.dp
            self.spot, self.across = take(s.row), take(s.dp)

        def start(self, parts):
            for index, value in enumerate(parts):
                where = ((index,) if self.lead else ()) + (slice(None), slice(None))
                self.whole[where] = value
                self.low[where] = value.astype(LOW)
            self.copies = []
            for step in dp.steps():
                view = self.low.at[self.lead + (span(dp.peer(step), self.size), slice(None))]
                self.copies.append(
                    remote(view, self.land.at[step], self.across + step, dp, dp.peer(step))
                )

        def spread(self):
            total = self.whole[self.lead + (span(h, self.size), slice(None))]
            for step, copy in zip(dp.steps(), self.copies):
                copy.wait_recv()
                total = total + self.land[step].astype(F32)
            self.mine[...] = total.astype(LOW)
            keep = self.lead + (slice(None),)
            self.last = []
            for other in row.steps():
                peer = row.peer(other)
                self.last.append(
                    remote(
                        self.mine.at[keep + (row_cols(peer),)],
                        self.out.at[self.lead + (r,)],
                        self.spot + other,
                        row,
                        peer,
                    )
                )
            self.out[self.lead + (r, slice(None), slice(None))] = self.mine[keep + (row_cols(r),)]

        def wait(self):
            wait_all(self.last)

    def squares_out(target, source):
        spot = take(s.row)
        copies = [
            remote(
                source.at[:, row_cols(row.peer(other))],
                target.at[span(r, s.rows), :],
                spot + other,
                row,
                row.peer(other),
            )
            for other in row.steps()
        ]
        target[span(r, s.rows), :] = source[:, row_cols(r)]
        return copies

    def rows_in(target, source):
        spot = take(s.row)
        copies = [
            remote(
                source.at[span(row.peer(other), s.rows), :],
                target.at[:, row_cols(r)],
                spot + other,
                row,
                row.peer(other),
            )
            for other in row.steps()
        ]
        target[:, row_cols(r)] = source[span(r, s.rows), :]
        return copies

    def all_reduce(ring, source, land):
        spot = take(ring.size)
        return [
            remote(source, land.at[step], spot + step, ring, ring.peer(step))
            for step in ring.steps()
        ]

    def landed(ring, total, land, copies):
        for step, copy in zip(ring.steps(), copies):
            copy.wait_recv()
            total = total + land[step]
        return total

    first = Gather(tmp.x_all, True)
    for b in blocks:
        first.start(b)
    mine = tmp.cot_all.at[span(c, s.tokens), row_cols(r)]
    spot = take(s.row)
    cot_square = [
        remote(mine, mine, spot + other, row, row.peer(other)) for other in row.steps()
    ]
    w_proj = Weight(tmp.s_proj, tmp.w_proj)
    spot = take(s.row)
    gain_copies = [
        remote(
            tmp.gains_own, tmp.gains_all.at[:, row_cols(r)], spot + other, row, row.peer(other)
        )
        for other in row.steps()
    ]
    tap_copies = all_reduce(dp, tmp.tap_own, tmp.tap_land)
    w_mixer = Weight(tmp.s_mixer, tmp.w_mixer)
    for b in blocks:
        first.forward(b)
    wait_all(cot_square)
    mine = tmp.cot_all.at[span(c, s.tokens), :]
    spot = take(s.col)
    cot_line = [
        remote(mine, mine, spot + step, col, col.peer(step)) for step in col.steps()
    ]
    w_proj.forward()
    w_mixer.forward()
    x_rows = rows_in(tmp.x_rows, ins.x)
    wait_all(gain_copies)
    taps = landed(dp, taps, tmp.tap_land, tap_copies)
    gain_one = tmp.gains_all[0:1, :]
    gain_two = tmp.gains_all[1:2, :]
    w_proj.wait()

    scatter_mixer = Scatter(tmp.m_out, tmp.m_one, tmp.m_mid, tmp.m_two)
    parts, mixed = tmp.parts, tmp.mixed
    length = s.length
    mixed[0:RIM, :] = jnp.zeros((RIM, s.chans), F32)
    for b in blocks:
        first.wait(b)
        value = tmp.x_all[block(b), :].astype(F32)
        mean = jnp.sum(value * value, axis=1, keepdims=True) / s.full
        low = (value * lax.rsqrt(mean + eps_norm) * gain_one).astype(LOW)
        tmp.normed_one[block(b), :] = low
        for part in range(3):
            parts[part, block(b), :] = contract_cols(low, tmp.w_proj[part])
        start = RIM + b * s.tokens
        mixed[start : start + s.tokens, :] = parts[0, block(b), :] * parts[2, block(b), :]
        convolved = jnp.zeros((s.tokens, s.chans), F32)
        for offset in range(KERNEL):
            at = start - HISTORY + offset
            convolved = convolved + taps[offset : offset + 1] * mixed[at : at + s.tokens, :]
        tmp.convolved[block(b), :] = convolved
        gated = (parts[1, block(b), :] * convolved).astype(LOW)
        tmp.gated[block(b), :] = gated
        if b == 0:
            w_mixer.wait()
        scatter_mixer.chunk(b, plain_product(gated, tmp.w_mixer[...]))

    w_up = Weight(tmp.s_up, tmp.w_up)
    w_down = Weight(tmp.s_down, tmp.w_down)
    cot_rows = rows_in(tmp.cot_rows, ins.cot)

    second = Gather(tmp.two_all, False)

    def norm_two(residual):
        mean = jnp.sum(residual * residual, axis=1, keepdims=True) / s.full
        return lax.rsqrt(mean + eps_norm)

    def own_two(b):
        @pl.when(c == b)
        def _():
            total = scatter_mixer.total(b)
            wait_all(x_rows)
            residual = tmp.x_rows[...] + total
            tmp.residual_two[...] = residual
            tmp.two_all[line(b), :] = (residual * norm_two(residual) * gain_two).astype(LOW)

        second.start(b)

    scatter_two = Scatter(tmp.b_out, tmp.b_one, tmp.b_mid, tmp.b_two)

    def ffn(b):
        second.wait(b)
        value = tmp.two_all[block(b), :]
        back = contract_cols(tmp.cot_all[block(b), :], tmp.w_down[...])
        gate_pre = contract_cols(value, tmp.w_up[0])
        lifted = contract_cols(value, tmp.w_up[1])
        sigmoid_gate = jax.nn.sigmoid(gate_pre)
        swish_gate = gate_pre * sigmoid_gate
        tmp.hidden[block(b), :] = (swish_gate * lifted).astype(LOW)
        gate_low = (
            back * lifted * sigmoid_gate * (1.0 + gate_pre * (1.0 - sigmoid_gate))
        ).astype(LOW)
        lift_low = (back * swish_gate).astype(LOW)
        tmp.d_gate[block(b), :] = gate_low
        tmp.d_lift[block(b), :] = lift_low
        scatter_two.chunk(
            b, plain_product(gate_low, tmp.w_up[0]) + plain_product(lift_low, tmp.w_up[1])
        )

    third = Gather(tmp.res_all, False)
    tmp.gain_part[...] = jnp.zeros(tmp.gain_part.shape, F32)

    def own_three(b):
        @pl.when(c == b)
        def _():
            d_normed = scatter_two.total(b)
            residual = tmp.residual_two[...]
            wait_all(cot_rows)
            inverse = norm_two(residual)
            scaled = d_normed * gain_two
            row_mean = jnp.sum(scaled * residual, axis=1, keepdims=True) / s.full
            d_residual = tmp.cot_rows[...] + inverse * (
                scaled - residual * inverse * inverse * row_mean
            )
            tmp.d_residual[...] = d_residual
            tmp.res_all[line(b), :] = d_residual.astype(LOW)
            tmp.gain_part[1:2, :] = jnp.sum(d_normed * residual * inverse, axis=0, keepdims=True)

        third.start(b)

    feed_z, feed_xy = take(s.col), take(s.row)
    feed_copies = {}

    def feed(step):
        at = span(col.peer(step) if step else c, s.tokens)
        partial = plain_product(tmp.hidden[at, :], tmp.w_down[...])
        tmp.f_out[step] = partial.astype(LOW)
        if step:
            feed_copies[step] = remote(
                tmp.f_out.at[step], tmp.f_land.at[step], feed_z + step, col, col.peer(step)
            )

    def feed_spread():
        total = tmp.f_out[0].astype(F32)
        for step, copy in feed_copies.items():
            copy.wait_recv()
            total = total + tmp.f_land[step].astype(F32)
        tmp.f_mid[...] = total.astype(LOW)
        return [
            remote(
                tmp.f_mid.at[:, row_cols(row.peer(other))],
                tmp.f_last.at[other],
                feed_xy + other,
                row,
                row.peer(other),
            )
            for other in row.steps()
        ]

    def feed_out(copies):
        wait_all(res_square)
        total = tmp.f_mid[:, row_cols(r)].astype(F32)
        for other, copy in zip(row.steps(), copies):
            copy.wait_recv()
            total = total + tmp.f_last[other].astype(F32)
        outs.block_output[...] = tmp.res_square[...] + total

    g_up = Gradient(tmp.gf_up, tmp.gb_up, tmp.gl_up, tmp.gs_up, outs.g_up)
    g_down = Gradient(tmp.gf_down, tmp.gb_down, tmp.gl_down, tmp.gs_down, outs.g_down)
    g_mixer = Gradient(tmp.gf_mixer, tmp.gb_mixer, tmp.gl_mixer, tmp.gs_mixer, outs.g_mixer)
    g_proj = Gradient(tmp.gf_proj, tmp.gb_proj, tmp.gl_proj, tmp.gs_proj, outs.g_proj)
    relay = scatter_mixer.relay
    relay(0)
    relay(1)
    own_two(0)
    relay(2)
    own_two(1)
    second.forward(0)
    relay(3)
    own_two(2)
    second.forward(1)
    own_two(3)
    second.forward(2)
    w_up.forward()
    w_down.forward()
    second.forward(3)
    wait_all(cot_line)
    w_up.wait()
    w_down.wait()
    ffn(0)
    ffn(1)
    ffn(2)
    scatter_two.relay(0)
    ffn(3)
    g_up.start(
        [
            contract_rows(tmp.d_gate[...], tmp.two_all[...]),
            contract_rows(tmp.d_lift[...], tmp.two_all[...]),
        ]
    )
    g_down.start([contract_rows(tmp.hidden[...], tmp.cot_all[...])])
    scatter_two.relay(1)
    own_three(0)
    g_up.spread()
    scatter_two.relay(2)
    own_three(1)
    third.forward(0)
    scatter_two.relay(3)
    own_three(2)
    third.forward(1)
    own_three(3)
    third.forward(2)
    third.forward(3)
    feed(3)
    feed(2)
    res_square = squares_out(tmp.res_square, tmp.residual_two)

    d_conv, d_proj = tmp.d_conv, tmp.d_proj
    d_conv[length : length + RIM, :] = jnp.zeros((RIM, s.chans), F32)
    scatter_one = Scatter(tmp.i_out, tmp.i_one, tmp.i_mid, tmp.i_two)

    def gate_back(b):
        third.wait(b)
        back = contract_cols(tmp.res_all[block(b), :], tmp.w_mixer[...])
        d_conv[block(b), :] = back * parts[1, block(b), :]
        d_proj[1, block(b), :] = (back * tmp.convolved[block(b), :]).astype(LOW)

    def conv_back(b):
        start = b * s.tokens
        d_mixed = jnp.zeros((s.tokens, s.chans), F32)
        for offset in range(KERNEL):
            tap = taps[HISTORY - offset : HISTORY - offset + 1]
            d_mixed = d_mixed + tap * d_conv[start + offset : start + offset + s.tokens, :]
        d_proj[0, block(b), :] = (d_mixed * parts[2, block(b), :]).astype(LOW)
        d_proj[2, block(b), :] = (d_mixed * parts[0, block(b), :]).astype(LOW)
        partial = plain_product(d_proj[0, block(b), :], tmp.w_proj[0])
        for part in range(1, 3):
            partial = partial + plain_product(d_proj[part, block(b), :], tmp.w_proj[part])
        scatter_one.chunk(b, partial)

    gate_back(0)
    gate_back(1)
    conv_back(0)
    gate_back(2)
    conv_back(1)
    gate_back(3)
    conv_back(2)
    conv_back(3)
    g_down.spread()

    scatter_one.relay(0)
    g_proj.start([contract_rows(d_proj[part], tmp.normed_one[...]) for part in range(3)])
    tmp.conv_part[...] = jnp.zeros(tmp.conv_part.shape, F32)
    for offset in range(KERNEL):
        start = RIM - HISTORY + offset
        tmp.conv_part[offset : offset + 1, :] = jnp.sum(
            d_conv[0:length, :] * mixed[start : start + length, :], axis=0, keepdims=True
        )
    conv_copies = all_reduce(dp, tmp.conv_part, tmp.conv_land)
    scatter_one.relay(1)
    g_proj.spread()
    scatter_one.relay(2)
    g_mixer.start([contract_rows(tmp.gated[...], tmp.res_all[...])])
    scatter_one.relay(3)
    feed(1)
    feed(0)
    g_mixer.spread()
    total = landed(dp, tmp.conv_part[...], tmp.conv_land, conv_copies)
    chosen = lax.dot_general(
        total,
        chooser((s.chans, s.stored_chan), 1),
        (((1,), (0,)), ((), ())),
        precision=lax.Precision.HIGHEST,
        preferred_element_type=F32,
    )
    tmp.conv_sum[...] = chosen
    conv_copies = all_reduce(row, tmp.conv_sum, tmp.conv_last)

    for b in blocks:

        @pl.when(c == b)
        def _(b=b):
            d_normed = scatter_one.total(b)
            value = tmp.x_rows[...]
            inverse = norm_two(value)
            tmp.gain_part[0:1, :] = jnp.sum(d_normed * value * inverse, axis=0, keepdims=True)
            scaled = d_normed * gain_one
            row_mean = jnp.sum(scaled * value, axis=1, keepdims=True) / s.full
            tmp.input_rows[...] = tmp.d_residual[...] + inverse * (
                scaled - value * inverse * inverse * row_mean
            )

    spot = take(s.row)
    gain_copies = [
        remote(
            tmp.gain_part.at[:, row_cols(row.peer(other))],
            tmp.gain_land_row.at[other],
            spot + other,
            row,
            row.peer(other),
        )
        for other in row.steps()
    ]
    input_copies = squares_out(outs.input_grad, tmp.input_rows)
    total = landed(row, tmp.gain_part[:, row_cols(r)], tmp.gain_land_row, gain_copies)
    tmp.gain_sum_row[...] = total
    gain_copies = all_reduce(col, tmp.gain_sum_row, tmp.gain_land_col)
    outs.g_conv[...] = landed(row, tmp.conv_sum[...], tmp.conv_last, conv_copies)
    feed_copies_row = feed_spread()
    total = landed(col, total, tmp.gain_land_col, gain_copies)
    tmp.gain_sum_col[...] = total
    gain_copies = all_reduce(dp, tmp.gain_sum_col, tmp.gain_land_dp)
    feed_out(feed_copies_row)
    outs.g_gains[...] = landed(dp, total, tmp.gain_land_dp, gain_copies)

    for gradient in (g_proj, g_mixer, g_up, g_down):
        gradient.wait()
    wait_all(input_copies)
    for copy in sent:
        copy.wait_send()
    for collective in (first, second, third, scatter_mixer, scatter_two, scatter_one):
        collective.finish()


def run_block(s, ins):
    outs = Names(
        block_output=((s.tokens, s.width), F32),
        input_grad=((s.tokens, s.width), F32),
        g_proj=((3, s.row, s.chan, s.width), LOW),
        g_mixer=((s.row, s.chan, s.width), LOW),
        g_up=((2, s.row, s.unit, s.width), LOW),
        g_down=((s.row, s.unit, s.width), LOW),
        g_conv=((8, s.stored_chan), F32),
        g_gains=((8, s.width), F32),
    )
    line = (s.rows, s.full)
    whole = ((s.length, s.full), LOW)
    out = ((s.col, s.tokens, s.full), LOW)
    one = ((s.col, s.row) + line, LOW)
    mid = ((s.col,) + line, LOW)
    small = ((8, s.chans), F32)
    tmp = Names(
        turned=((3, s.stored_chan, s.width), F32),
        s_proj=((3, s.row, s.chan, s.width), LOW),
        s_mixer=((s.row, s.chan, s.width), LOW),
        s_up=((2, s.row, s.unit, s.width), LOW),
        s_down=((s.row, s.unit, s.width), LOW),
        gains_own=((8, s.width), F32),
        gains_all=((8, s.full), F32),
        tap_own=small,
        tap_land=((s.dp, 8, s.chans), F32),
        w_proj=((3, s.chans, s.full), LOW),
        w_mixer=((s.chans, s.full), LOW),
        w_up=((2, s.units, s.full), LOW),
        w_down=((s.units, s.full), LOW),
        x_all=whole,
        cot_all=whole,
        two_all=whole,
        res_all=whole,
        normed_one=whole,
        m_out=out,
        m_one=one,
        m_mid=mid,
        m_two=mid,
        b_out=out,
        b_one=one,
        b_mid=mid,
        b_two=mid,
        i_out=out,
        i_one=one,
        i_mid=mid,
        i_two=mid,
        f_out=out,
        f_land=out,
        f_mid=((s.tokens, s.full), LOW),
        f_last=((s.row, s.tokens, s.width), LOW),
        res_square=((s.tokens, s.width), F32),
        x_rows=(line, F32),
        cot_rows=(line, F32),
        residual_two=(line, F32),
        d_residual=(line, F32),
        input_rows=(line, F32),
        parts=((3, s.length, s.chans), F32),
        mixed=((s.length + RIM, s.chans), F32),
        convolved=((s.length, s.chans), F32),
        gated=((s.length, s.chans), LOW),
        hidden=((s.length, s.units), LOW),
        d_gate=((s.length, s.units), LOW),
        d_lift=((s.length, s.units), LOW),
        d_conv=((s.length + RIM, s.chans), F32),
        d_proj=((3, s.length, s.chans), LOW),
        conv_part=small,
        conv_land=((s.dp, 8, s.chans), F32),
        conv_sum=((8, s.stored_chan), F32),
        conv_last=((s.row, 8, s.stored_chan), F32),
        gain_part=((8, s.full), F32),
        gain_land_row=((s.row, 8, s.width), F32),
        gain_sum_row=((8, s.width), F32),
        gain_land_col=((s.col, 8, s.width), F32),
        gain_sum_col=((8, s.width), F32),
        gain_land_dp=((s.dp, 8, s.width), F32),
        gf_proj=((3, s.chans, s.full), F32),
        gb_proj=((3, s.chans, s.full), LOW),
        gl_proj=((s.dp, 3, s.chan, s.full), LOW),
        gs_proj=((3, s.chan, s.full), LOW),
        gf_mixer=((s.chans, s.full), F32),
        gb_mixer=((s.chans, s.full), LOW),
        gl_mixer=((s.dp, s.chan, s.full), LOW),
        gs_mixer=((s.chan, s.full), LOW),
        gf_up=((2, s.units, s.full), F32),
        gb_up=((2, s.units, s.full), LOW),
        gl_up=((s.dp, 2, s.unit, s.full), LOW),
        gs_up=((2, s.unit, s.full), LOW),
        gf_down=((s.units, s.full), F32),
        gb_down=((s.units, s.full), LOW),
        gl_down=((s.dp, s.unit, s.full), LOW),
        gs_down=((s.unit, s.full), LOW),
    )

    def kernel(*refs):
        n_in, n_out = len(ins.items), len(outs.items)
        scratch = tmp.bound(refs[n_in + n_out :])
        scratch.arguments = refs[-3 - n_in : -3]
        block_kernel(
            s,
            ins.bound(refs[:n_in]),
            outs.bound(refs[n_in : n_in + n_out]),
            scratch,
            *refs[-3:],
        )

    results = pl.pallas_call(
        kernel,
        out_shape=[jax.ShapeDtypeStruct(*spec) for spec in outs.items.values()],
        in_specs=[pl.BlockSpec(memory_space=pl.ANY)] * len(ins.items),
        out_specs=[pl.BlockSpec(memory_space=pltpu.VMEM)] * len(outs.items),
        scratch_shapes=[pltpu.VMEM(*spec) for spec in tmp.items.values()]
        + [pltpu.VMEM(x.shape, x.dtype) for x in ins.items.values()]
        + [
            pltpu.SemaphoreType.DMA((s.spots,)),
            pltpu.SemaphoreType.DMA((s.spots,)),
            pltpu.SemaphoreType.DMA((4 + len(ins.items),)),
        ],
        compiler_params=pltpu.CompilerParams(
            collective_id=0, has_side_effects=True, vmem_limit_bytes=VMEM_LIMIT
        ),
    )(*ins.items.values())
    return outs.bound(results)


def update_kernel(s, small, grads, outs, refs, big_in, big_out, in_sem, out_sem):
    chunks = []
    for part in range(3):
        chunks.append((0, part, slice(None), s.stored_chan))
    for index, lead, kept in ((1, 0, s.cut_chan), (2, 2, s.cut_unit), (3, 0, s.cut_unit)):
        for first in range(max(lead, 1)):
            chunks.append((index, first if lead else None, slice(None), kept))

    def views(ref, first, moments):
        where = ((slice(None),) if moments else ()) + (() if first is None else (first,))
        return ref.at[where] if where else ref

    count = len(chunks)
    reads = []
    for k, (index, first, _, _) in enumerate(chunks):
        pair = []
        for kind in range(2):
            copy = pltpu.make_async_copy(
                views(refs[kind * 4 + index], first, kind),
                views(big_in[kind * 4 + index], first, kind),
                in_sem.at[kind * count + k],
            )
            copy.start()
            pair.append(copy)
        reads.append(pair)
    writes = []

    def gradient(index, first, kept):
        source = grads[index]
        pieces = []
        for part in range(s.row):
            where = (part,) if first is None else (first, part)
            pieces.append(source[where + (pl.ds(0, kept), slice(None))].astype(F32))
        return jnp.concatenate(pieces, axis=0)

    for k, (index, first, _, kept) in enumerate(chunks):
        for copy in reads[k]:
            copy.wait()
        if index == 0:
            value = gradient(0, first, s.cut_chan).T
        else:
            value = gradient(index, first, kept)
        where = () if first is None else (first,)
        full = (slice(None), slice(None))
        weight, moments = big_in[index], big_in[4 + index]
        new, one, two = adam(
            weight[where + full],
            value,
            moments[(0,) + where + full],
            moments[(1,) + where + full],
            matrix_rate,
            decay_rate,
        )
        big_out[index][where + full] = value
        big_out[4 + index][where + full] = new
        big_out[8 + index][(0,) + where + full] = one
        big_out[8 + index][(1,) + where + full] = two
        for kind in range(3):
            copy = pltpu.make_async_copy(
                views(big_out[kind * 4 + index], first, kind == 2),
                views(outs[kind * 4 + index], first, kind == 2),
                out_sem.at[kind * count + k],
            )
            copy.start()
            writes.append(copy)

    g_conv = small.g_conv[0:KERNEL, :]
    new, one, two = adam(
        small.conv[...], g_conv, small.conv_m[:, 0, :], small.conv_m[:, 1, :], small_rate, 0.0
    )
    small.conv_grad[...] = g_conv
    small.conv_new[...] = new
    small.conv_m_new[:, 0, :] = one
    small.conv_m_new[:, 1, :] = two
    g_gains = small.g_gains[0:2, :]
    new, one, two = adam(
        small.gains[...], g_gains, small.gains_m[0], small.gains_m[1], small_rate, 0.0
    )
    small.gains_grad[...] = g_gains
    small.gains_new[...] = new
    small.gains_m_new[0] = one
    small.gains_m_new[1] = two
    small.out_one[...] = small.in_one[...]
    small.out_two[...] = small.in_two[...]
    for copy in writes:
        copy.wait()


def run_update(s, small_in, grads, weights, moments):
    small_out = Names(
        conv_grad=small_in.conv,
        conv_new=small_in.conv,
        conv_m_new=small_in.conv_m,
        gains_grad=small_in.gains,
        gains_new=small_in.gains,
        gains_m_new=small_in.gains_m,
        out_one=small_in.in_one,
        out_two=small_in.in_two,
    )
    n_small, n_out = len(small_in.items), len(small_out.items)
    count = 3 + 1 + 2 + 1
    like = [jax.ShapeDtypeStruct(x.shape, x.dtype) for x in small_out.items.values()]
    big = [jax.ShapeDtypeStruct(x.shape, F32) for x in weights + weights + moments]

    def kernel(*refs):
        refs = list(refs)

        def grab(size):
            taken = refs[:size]
            del refs[:size]
            return taken

        names_in = grab(n_small)
        g = grab(4)
        hbm = grab(8)
        names_out = grab(n_out)
        outs = grab(12)
        big_in, big_out = grab(8), grab(12)
        small = Names(
            **dict(zip(small_in.items, names_in)), **dict(zip(small_out.items, names_out))
        )
        update_kernel(s, small, g, outs, hbm, big_in, big_out, *refs)

    vmem, here = pl.BlockSpec(memory_space=pltpu.VMEM), pl.BlockSpec(memory_space=pl.ANY)
    results = pl.pallas_call(
        kernel,
        out_shape=like + big,
        in_specs=[vmem] * (n_small + 4) + [here] * 8,
        out_specs=[vmem] * n_out + [here] * 12,
        scratch_shapes=[pltpu.VMEM(x.shape, F32) for x in weights + moments]
        + [pltpu.VMEM(x.shape, F32) for x in big]
        + [pltpu.SemaphoreType.DMA((2 * count,)), pltpu.SemaphoreType.DMA((3 * count,))],
        compiler_params=pltpu.CompilerParams(vmem_limit_bytes=VMEM_LIMIT),
    )(*small_in.items.values(), *grads, *weights, *moments)
    return small_out.bound(results[:n_out]), results[n_out:]


def on_device(
    block_input,
    out_cot,
    proj_weight,
    conv_weight,
    mixer_weight,
    up_weight,
    down_weight,
    norm_gains,
    proj_moments,
    conv_moments,
    mixer_moments,
    up_moments,
    down_moments,
    gains_moments,
):
    sizes = tuple(lax.axis_size(axis) for axis in ("dp", "row", "col"))
    s = Shapes(sizes, *block_input.shape, proj_weight.shape[2], up_weight.shape[2])
    proj_turned = proj_weight.transpose(1, 0, 2)
    up_turned = up_weight.transpose(1, 2, 0)
    ins = Names(
        x=block_input,
        cot=out_cot,
        gains=norm_gains,
        taps=conv_weight,
        proj=proj_turned,
        mixer=mixer_weight,
        up=up_turned,
        down=down_weight,
    )
    out = run_block(s, ins)
    small_in = Names(
        conv=conv_weight,
        conv_m=conv_moments.transpose(1, 0, 2),
        gains=norm_gains,
        gains_m=gains_moments,
        g_conv=out.g_conv,
        g_gains=out.g_gains,
        in_one=out.block_output,
        in_two=out.input_grad,
    )
    small, big = run_update(
        s,
        small_in,
        [out.g_proj, out.g_mixer, out.g_up, out.g_down],
        [proj_turned, mixer_weight, up_turned, down_weight],
        [
            proj_moments.transpose(0, 2, 1, 3),
            mixer_moments,
            up_moments.transpose(0, 2, 3, 1),
            down_moments,
        ],
    )
    grads, news, moments = big[:4], big[4:8], big[8:]

    def weights_of(values, taps, gains):
        return (
            values[0].transpose(1, 0, 2),
            taps,
            values[1],
            values[2].transpose(2, 0, 1),
            values[3],
            gains,
        )

    return (
        (small.out_one, small.out_two)
        + weights_of(grads, small.conv_grad, small.gains_grad)
        + weights_of(news, small.conv_new, small.gains_new)
        + (
            moments[0].transpose(0, 2, 1, 3),
            small.conv_m_new.transpose(1, 0, 2),
            moments[1],
            moments[2].transpose(0, 3, 1, 2),
            moments[3],
            small.gains_m_new,
        )
    )


def solution(mesh):
    tokens = P(("dp", "col"), "row")
    by_width = P("row", None, ("dp", "col"))
    by_unit = P(("dp", "col"), "row")
    taps = P(None, ("dp", "col"))
    gains = P(None, "row")
    weights = (by_width, taps, by_unit, by_width, by_unit, gains)
    stacked = tuple(P(None, *spec) for spec in weights)
    return jax.shard_map(
        on_device,
        mesh=mesh,
        in_specs=(tokens, tokens) + weights + stacked,
        out_specs=(tokens, tokens) + weights + weights + stacked,
        check_vma=False,
    )
```

time: 257 us -> 140 us (0.54)
  other arithmetic: 42.3 us -> 0 us
  Pallas kernels: 180 us -> 139 us
  matrix products: 23.6 us -> 0 us
  local copies, waits for them, and re-layouts: 8.95 us -> 0 us
    pallas_call x15 -> x2, Pallas kernels: 180 us -> 139 us  [the longest x1 130 us: run_block(): pl.pallas_call(kernel, out_shape=[jax.ShapeDtypeStruct(*spec) for spec in...]
    dot_general x18 -> x0, matrix products: 23.6 us -> none  [the longest x6 8.74 us: plain_product(): return jnp.dot(left_side, right_side, preferred_element_type=jnp.float32)]
    convert_element_type x11 -> x0, other arithmetic: 9.97 us -> none  [the longest x1 2.08 us: on_device(): hidden = (swish_gate * lifted).astype(low)]
    reduce_sum x5 -> x0, other arithmetic: 7.46 us -> none  [the longest x1 2.43 us: gain_sums(): return jnp.sum(d_normed * residual * inverse, axis=0)]
    select_n x8 -> x0, other arithmetic: 6.98 us -> none  [the longest x6 6.25 us: adam_step(): jnp.where(is_first, beta_first * moments + (1.0 - beta_first) * gradient[...]
    mul x7 -> x0, other arithmetic: 4.82 us -> none  [the longest x3 3.56 us: adam_step(): (1.0 - beta_second) * gradient * gradient]
    add x12 -> x0, other arithmetic: 4.03 us -> none  [the longest x6 1.7 us: added(): total = total + blocks[index].astype(jnp.float32)]
    unnamed x118 -> x0, local copies, waits for them, and re-layouts: 3.85 us -> none
where the time goes in v1:
time: 140 us
  Pallas kernels  139 us (99%)
    pallas_call x1, Pallas kernels, run_block(): pl.pallas_call(kernel, out_shape=[jax.ShapeDtypeStruct(*spec) for spec in...  130 us
    pallas_call x1, Pallas kernels, run_update(): pl.pallas_call(kernel, out_shape=like + big, in_specs=[vmem] * (n_small +...  9.22 us

profile of v1, /device:TPU:0, one launch (start us, length us, event | category | flops | bytes accessed | tf_op | source)
XLA Modules:
  0.0 139.6 jit_solution(3510477304544580175)
XLA Ops:
  0.7 129.5 %shard_map.293 = (f32[128,256]{1,0:T(8,128)}, f32[128,256]{1,0:T(8,128)}, bf16[3,4,32,256]{3,2,1,0:T(8,128)(2,1)}, bf16[4,32,256]{2,1,0:T(8,128)(2,1)}, bf16[2,4...) custom-call(f32[128,256]{1,0:T(8,128)} %refs_0_.2, ...), custom_call_target="tpu_custom_call" | custom-call | tf_op jit(solution)/shard_map/pallas_call | solution.py:862
  130.2 9.2 %shard_map.294 = (f32[3,128]{1,0:T(4,128)}, f32[3,128]{1,0:T(4,128)}, f32[3,2,128]{2,1,0:T(2,128)}, f32[2,256]{1,0:T(2,128)}, f32[2,256]{1,0:T(2,128)}, /*index=...) custom-call(f32[3,128]{1,0:T(4,128)} %refs_0_.3, ...), custom_call_target="tpu_custom_call" | custom-call | tf_op jit(solution)/shard_map/pallas_call | solution.py:1005

commit v2 on v1

--- a/solution.py
+++ b/solution.py
@@ -456,11 +456,13 @@
     for b in blocks:
         first.forward(b)
     wait_all(cot_square)
-    mine = tmp.cot_all.at[span(c, s.tokens), :]
-    spot = take(s.col)
-    cot_line = [
-        remote(mine, mine, spot + step, col, col.peer(step)) for step in col.steps()
-    ]
+    cot_spot = take(s.col)
+
+    def cot_send(step):
+        mine = tmp.cot_all.at[span(c, s.tokens), :]
+        return remote(mine, mine, cot_spot + step, col, col.peer(step))
+
+    cot_line = [cot_send(step) for step in col.steps()]
     w_proj.forward()
     w_mixer.forward()
     x_rows = rows_in(tmp.x_rows, ins.x)
@@ -599,29 +601,20 @@
     g_down = Gradient(tmp.gf_down, tmp.gb_down, tmp.gl_down, tmp.gs_down, outs.g_down)
     g_mixer = Gradient(tmp.gf_mixer, tmp.gb_mixer, tmp.gl_mixer, tmp.gs_mixer, outs.g_mixer)
     g_proj = Gradient(tmp.gf_proj, tmp.gb_proj, tmp.gl_proj, tmp.gs_proj, outs.g_proj)
-    relay = scatter_mixer.relay
-    relay(0)
-    relay(1)
-    own_two(0)
-    relay(2)
-    own_two(1)
-    second.forward(0)
-    relay(3)
-    own_two(2)
-    second.forward(1)
-    own_two(3)
-    second.forward(2)
+    for b in blocks:
+        scatter_mixer.relay(b)
+    for b in blocks:
+        own_two(b)
+    for b in blocks:
+        second.forward(b)
+    w_down.forward()
     w_up.forward()
-    w_down.forward()
-    second.forward(3)
     wait_all(cot_line)
+    w_down.wait()
     w_up.wait()
-    w_down.wait()
-    ffn(0)
-    ffn(1)
-    ffn(2)
+    for b in blocks:
+        ffn(b)
     scatter_two.relay(0)
-    ffn(3)
     g_up.start(
         [
             contract_rows(tmp.d_gate[...], tmp.two_all[...]),
@@ -629,20 +622,15 @@
         ]
     )
     g_down.start([contract_rows(tmp.hidden[...], tmp.cot_all[...])])
-    scatter_two.relay(1)
-    own_three(0)
+    for b in range(1, s.col):
+        scatter_two.relay(b)
+    for b in blocks:
+        own_three(b)
     g_up.spread()
-    scatter_two.relay(2)
-    own_three(1)
-    third.forward(0)
-    scatter_two.relay(3)
-    own_three(2)
-    third.forward(1)
-    own_three(3)
-    third.forward(2)
-    third.forward(3)
-    feed(3)
-    feed(2)
+    for b in blocks:
+        third.forward(b)
+    for step in range(s.col - 1, 1, -1):
+        feed(step)
     res_square = squares_out(tmp.res_square, tmp.residual_two)
 
     d_conv, d_proj = tmp.d_conv, tmp.d_proj
@@ -667,15 +655,25 @@
         for part in range(1, 3):
             partial = partial + plain_product(d_proj[part, block(b), :], tmp.w_proj[part])
         scatter_one.chunk(b, partial)
+        normed = tmp.normed_one[block(b), :].astype(F32)
+        tmp.gain_part[0:1, :] += jnp.sum(partial * normed, axis=0, keepdims=True) / gain_one
 
     gate_back(0)
-    gate_back(1)
-    conv_back(0)
-    gate_back(2)
-    conv_back(1)
-    gate_back(3)
-    conv_back(2)
-    conv_back(3)
+    for b in range(1, s.col):
+        gate_back(b)
+        conv_back(b - 1)
+    conv_back(s.col - 1)
+    spot = take(s.row)
+    gain_copies = [
+        remote(
+            tmp.gain_part.at[:, row_cols(row.peer(other))],
+            tmp.gain_land_row.at[other],
+            spot + other,
+            row,
+            row.peer(other),
+        )
+        for other in row.steps()
+    ]
     g_down.spread()
 
     scatter_one.relay(0)
@@ -689,9 +687,13 @@
     conv_copies = all_reduce(dp, tmp.conv_part, tmp.conv_land)
     scatter_one.relay(1)
     g_proj.spread()
-    scatter_one.relay(2)
+    for b in range(2, s.col - 1):
+        scatter_one.relay(b)
     g_mixer.start([contract_rows(tmp.gated[...], tmp.res_all[...])])
-    scatter_one.relay(3)
+    scatter_one.relay(s.col - 1)
+    gain_total = landed(row, tmp.gain_part[:, row_cols(r)], tmp.gain_land_row, gain_copies)
+    tmp.gain_sum_row[...] = gain_total
+    gain_copies = all_reduce(col, tmp.gain_sum_row, tmp.gain_land_col)
     feed(1)
     feed(0)
     g_mixer.spread()
@@ -713,31 +715,16 @@
             d_normed = scatter_one.total(b)
             value = tmp.x_rows[...]
             inverse = norm_two(value)
-            tmp.gain_part[0:1, :] = jnp.sum(d_normed * value * inverse, axis=0, keepdims=True)
             scaled = d_normed * gain_one
             row_mean = jnp.sum(scaled * value, axis=1, keepdims=True) / s.full
             tmp.input_rows[...] = tmp.d_residual[...] + inverse * (
                 scaled - value * inverse * inverse * row_mean
             )
 
-    spot = take(s.row)
-    gain_copies = [
-        remote(
-            tmp.gain_part.at[:, row_cols(row.peer(other))],
-            tmp.gain_land_row.at[other],
-            spot + other,
-            row,
-            row.peer(other),
-        )
-        for other in row.steps()
-    ]
     input_copies = squares_out(outs.input_grad, tmp.input_rows)
-    total = landed(row, tmp.gain_part[:, row_cols(r)], tmp.gain_land_row, gain_copies)
-    tmp.gain_sum_row[...] = total
-    gain_copies = all_reduce(col, tmp.gain_sum_row, tmp.gain_land_col)
     outs.g_conv[...] = landed(row, tmp.conv_sum[...], tmp.conv_last, conv_copies)
     feed_copies_row = feed_spread()
-    total = landed(col, total, tmp.gain_land_col, gain_copies)
+    total = landed(col, gain_total, tmp.gain_land_col, gain_copies)
     tmp.gain_sum_col[...] = total
     gain_copies = all_reduce(dp, tmp.gain_sum_col, tmp.gain_land_dp)
     feed_out(feed_copies_row)

time: 140 us -> 135 us (0.964)
  Pallas kernels: 139 us -> 133 us
    pallas_call x1, Pallas kernels: 130 us -> 124 us  [run_block(): pl.pallas_call(kernel, out_shape=[jax.ShapeDtypeStruct(*spec) for spec in...]
where the time goes in v2:
time: 135 us; the launch traced here: 134 us
  Pallas kernels  133 us (99%)
    pallas_call x1, Pallas kernels, run_block(): pl.pallas_call(kernel, out_shape=[jax.ShapeDtypeStruct(*spec) for spec in...  124 us
    pallas_call x1, Pallas kernels, run_update(): pl.pallas_call(kernel, out_shape=like + big, in_specs=[vmem] * (n_small +...  9.22 us

profile of v2, /device:TPU:0, one launch (start us, length us, event | category | flops | bytes accessed | tf_op | source)
XLA Modules:
  0.0 134.1 jit_solution(17285103611237455647)
XLA Ops:
  0.7 124.0 %shard_map.293 = (f32[128,256]{1,0:T(8,128)}, f32[128,256]{1,0:T(8,128)}, bf16[3,4,32,256]{3,2,1,0:T(8,128)(2,1)}, bf16[4,32,256]{2,1,0:T(8,128)(2,1)}, bf16[2,4...) custom-call(f32[128,256]{1,0:T(8,128)} %refs_0_.2, ...), custom_call_target="tpu_custom_call" | custom-call | tf_op jit(solution)/shard_map/pallas_call | solution.py:849
  124.7 9.2 %shard_map.294 = (f32[3,128]{1,0:T(4,128)}, f32[3,128]{1,0:T(4,128)}, f32[3,2,128]{2,1,0:T(2,128)}, f32[2,256]{1,0:T(2,128)}, f32[2,256]{1,0:T(2,128)}, /*index=...) custom-call(f32[3,128]{1,0:T(4,128)} %refs_0_.3, ...), custom_call_target="tpu_custom_call" | custom-call | tf_op jit(solution)/shard_map/pallas_call | solution.py:992
